TPU v7x, 32 devices: a whole 2x2x4 slice. The times are simulated.
32 devices in a mesh: rep: 4 (over y, x), shard: 8 (over z, core).
Axes of the slice: x: 2, y: 2, z: 4, core: 2. Of those that a mesh axis runs over, the one named last changes fastest.
Arguments:
- anchor_attn: float32 [2048, 2048], P('shard')
- anchor_ffn: float32 [2048, 5120], P('shard')
- local_attn: float32 [4, 2048, 2048], P('rep', 'shard'), as said below
- local_ffn: float32 [4, 2048, 5120], P('rep', 'shard'), as said below
Outputs:
- outer_attn: float32 [2048, 2048], P('shard')
- outer_ffn: float32 [2048, 5120], P('shard')
Inputs may be any that keep to these rules, and one draw needn't show every extreme that they name: `local_attn`: every replica's weights differ from the anchor. `local_ffn`: every replica's weights differ from the anchor.
All inputs are finite; a program needn't handle non-finite values.
Results may differ from a plain program's by a relative error of at most 0.0003.
Values sent between devices are 32-bit elements; how exact they have to be, the bound alone decides.
A program may use at most 64 MiB of HBM per device.

v0:
```python
import jax
import jax.numpy as jnp
from jax import lax
from jax.sharding import PartitionSpec as P


def own_squares(partial_value):
    return lax.psum(partial_value, "shard")


def clip_factor(squares):
    return jnp.minimum(jnp.float32(1.0), 1.0 / jnp.sqrt(squares))


def shards(anchor_attn, anchor_ffn, local_attn, local_ffn):
    replicas = lax.axis_size("rep")
    delta_attn = local_attn[0] - anchor_attn
    delta_ffn = local_ffn[0] - anchor_ffn
    partial_value = jnp.sum(delta_attn * delta_attn) + jnp.sum(delta_ffn * delta_ffn)
    moved_attn, moved_ffn = (
        lax.all_to_all(delta_attn[None], "rep", split_axis=1, concat_axis=0, tiled=True),
        lax.all_to_all(delta_ffn[None], "rep", split_axis=1, concat_axis=0, tiled=True),
    )
    factor = clip_factor(own_squares(partial_value))
    factors = lax.all_gather(factor[None], "rep", axis=0, tiled=True)
    summed_attn = jnp.sum(factors[:, None, None] * moved_attn, axis=0)
    summed_ffn = jnp.sum(factors[:, None, None] * moved_ffn, axis=0)
    fresh_attn = summed_attn / replicas
    fresh_ffn = summed_ffn / replicas
    outer_attn, outer_ffn = (
        lax.all_gather(fresh_attn, "rep", axis=0, tiled=True),
        lax.all_gather(fresh_ffn, "rep", axis=0, tiled=True),
    )
    return (outer_attn, outer_ffn)


def solution(mesh):
    placed = (P("shard", None), P("shard", None), P("rep", "shard", None), P("rep", "shard", None))
    return jax.shard_map(
        shards,
        mesh=mesh,
        in_specs=placed,
        out_specs=(P("shard", None), P("shard", None)),
        check_vma=False,
    )
```

profile of v0, /device:TPU:0, one launch (start us, length us, event | category | flops | bytes accessed | tf_op | source)
XLA Modules:
  0.0 226.7 jit_solution(9574172654774050802)
XLA Ops:
  7.2 3.4 %multiply_reduce_fusion.3 = (f32[]{:T(128)}, f32[256,2048]{1,0:T(8,128)S(1)}) fusion(f32[256,2048]{1,0:T(8,128)} %param.4, f32[1,256,2048]{2,1,0:T(8,128)} %param.6), kind=kLoop, calls=%fused_computation.5 | loop fusion | flops 1572863 | bytes 6291460 | tf_op jit(solution)/shard_map/reduce_sum | solution.py:19
  10.6 2.8 %broadcast_in_dim.12 = f32[1,256,2048]{2,0,1:T(1,128)} reshape(f32[256,2048]{1,0:T(8,128)S(1)} %get-tuple-element.5) | data formatting | bytes 4194304 | tf_op jit(solution)/shard_map/broadcast_in_dim | solution.py:21
  13.4 5.2 %all-to-all-start = ((f32[1,256,2048]{2,0,1:T(1,128)}), f32[1,256,2048]{2,0,1:T(1,128)S(1)}, u32[]{:S(2)}, u32[]{:S(2)}) async-start(f32[1,256,2048]{2,0,1:T(1,128)} %broadcast_in_dim.12), calls=%async_computation | async-start | bytes 4194304 | tf_op jit(solution)/shard_map/all_to_all | solution.py:21
  18.6 6.1 %multiply_reduce_fusion.1 = (f32[]{:T(128)}, f32[256,5120]{1,0:T(8,128)S(1)}) fusion(f32[256,5120]{1,0:T(8,128)} %param.5, f32[1,256,5120]{2,1,0:T(8,128)} %param.7), kind=kLoop, calls=%fused_computation.2 | loop fusion | flops 3932159 | bytes 15728644 | tf_op jit(solution)/shard_map/reduce_sum | solution.py:19
  24.7 4.6 %broadcast_in_dim.13 = f32[1,256,5120]{2,0,1:T(1,128)} reshape(f32[256,5120]{1,0:T(8,128)S(1)} %get-tuple-element.3) | data formatting | bytes 10485760 | tf_op jit(solution)/shard_map/broadcast_in_dim | solution.py:22
  29.3 0.0 copy-start
  29.3 14.1 %all-to-all-done = f32[1,256,2048]{2,0,1:T(1,128)S(1)} async-done(((f32[1,256,2048]{2,0,1:T(1,128)}), f32[1,256,2048]{2,0,1:T(1,128)S(1)}, u32[]{:S(2)}, u32[]{:S(2)}) %all-to-all-start) | async-done | bytes 2097184 | tf_op jit(solution)/shard_map/all_to_all | solution.py:21
  43.4 5.0 %all-to-all-start.1 = ((f32[1,256,5120]{2,0,1:T(1,128)}), f32[1,256,5120]{2,0,1:T(1,128)}, u32[]{:S(2)}, u32[]{:S(2)}) async-start(f32[1,256,5120]{2,0,1:T(1,128)} %broadcast_in_dim.13), calls=%async_computation.1 | async-start | bytes 10485760 | tf_op jit(solution)/shard_map/all_to_all | solution.py:22
  48.5 0.0 all-gather.3.cloned.1.call-start
  49.8 16.5 %psum.7 = f32[]{:T(128)} all-reduce(f32[]{:T(128)S(6)} %add.5), channel_id=1, replica_groups=mesh['rep'=4,'shard'=8] {'shard'}, use_global_device_ids=true, to_apply=%region_2.0 | all-reduce | flops 1 | bytes 8 | tf_op jit(solution)/shard_map/psum | solution.py:8
  67.0 0.0 copy-done
  67.0 0.6 dynamic-slice
  67.6 0.7 dynamic-update-slice
  68.3 41.3 %all-reduce = f32[4]{0:T(128)S(1)} all-reduce(f32[4]{0:T(128)S(1)} %dynamic-update-slice), channel_id=1, replica_groups=mesh['rep'=4,'shard'=8] {'rep'}, use_global_device_ids=true, to_apply=%add | all-reduce | flops 4 | bytes 32
  109.7 0.9 copy.6
  110.6 0.3 multiply_reduce_fusion.2
  110.8 0.8 broadcast_multiply_fusion.1
  111.7 0.0 all-gather.3.cloned.1.call-update
  111.7 0.0 all-gather.5.cloned.1.call-start
  111.8 0.0 all-to-all-done.1
  111.8 3.4 %copy.7 = f32[1,256,5120]{2,1,0:T(8,128)S(1)} copy(f32[1,256,5120]{2,0,1:T(1,128)} %all-to-all-done.1) | data formatting | bytes 10485760
  115.2 0.7 multiply_reduce_fusion
  115.9 1.2 broadcast_multiply_fusion
  117.0 0.0 all-gather.5.cloned.1.call-update
  117.1 30.5 %all-gather.3.cloned.1.call-done = f32[256,2048]{1,0:T(8,128)} async-done(((f32[64,2048]{1,0:T(8,128)}), f32[256,2048]{1,0:T(8,128)}) %all-gather.3.cloned.1.call-update) | async-done | bytes 2097168 | tf_op jit(solution)/shard_map/all_gather | solution.py:31
  147.6 63.7 %all-gather.5.cloned.1.call-done = f32[256,5120]{1,0:T(8,128)} async-done(((f32[64,5120]{1,0:T(8,128)}), f32[256,5120]{1,0:T(8,128)}) %all-gather.5.cloned.1.call-update) | async-done | bytes 5242896 | tf_op jit(solution)/shard_map/all_gather | solution.py:32
  211.3 3.1 %copy.11 = f32[256,2048]{1,0:T(8,128)} copy(f32[256,2048]{1,0:T(8,128)} %all-gather.3.cloned.1.call-done) | data formatting | bytes 4194304
  214.5 5.4 %copy.12 = f32[256,5120]{1,0:T(8,128)} copy(f32[256,5120]{1,0:T(8,128)} %all-gather.5.cloned.1.call-done) | data formatting | bytes 10485760
  (1 shorter events, 0.0 us)
Async XLA Ops:
  13.4 30.1 %all-to-all-start = ((f32[1,256,2048]{2,0,1:T(1,128)}), f32[1,256,2048]{2,0,1:T(1,128)S(1)}, u32[]{:S(2)}, u32[]{:S(2)}) async-start(f32[1,256,2048]{2,0,1:T(1,128)} %broadcast_in_dim.12), calls=%async_computation | async-start | bytes 4194304 | tf_op jit(solution)/shard_map/all_to_all | solution.py:21
  29.3 37.7 %copy-start = (u32[32]{0:T(128)S(1)}, u32[32]{0:T(128)}, u32[]{:S(2)}) copy-start(u32[32]{0:T(128)} %constant.13) | copy-start | bytes 388
  43.4 68.3 %all-to-all-start.1 = ((f32[1,256,5120]{2,0,1:T(1,128)}), f32[1,256,5120]{2,0,1:T(1,128)}, u32[]{:S(2)}, u32[]{:S(2)}) async-start(f32[1,256,5120]{2,0,1:T(1,128)} %broadcast_in_dim.13), calls=%async_computation.1 | async-start | bytes 10485760 | tf_op jit(solution)/shard_map/all_to_all | solution.py:22
  48.5 99.1 %all-gather.3.cloned.1.call-start = ((), (), s32[]{:S(2)}) async-start(), calls=%async_computation.2 | async-start | bytes 2621440 | tf_op jit(solution)/shard_map/all_gather | solution.py:31
  111.7 99.6 %all-gather.5.cloned.1.call-start = ((), (), s32[]{:S(2)}) async-start(), calls=%async_computation.3 | async-start | bytes 6553600 | tf_op jit(solution)/shard_map/all_gather | solution.py:32
Sparse Core Ops, SparseCore 0:
  111.8 35.7 all-gather.2
  150.0 61.2 all-gather.4
where the time goes:
time: 227 us
  waiting for transfers between devices  108 us (48%)
  blocking collectives  57.8 us (25%)
  local copies, waits for them, and re-layouts  21.6 us (10%)
  between operations  16 us (7%)
  other arithmetic  12.5 us (6%)
  starting transfers between devices  10.3 us (5%)
    all_gather x1, waiting for transfers between devices, shards(): lax.all_gather(fresh_ffn, 'rep', axis=0, tiled=True)  63.7 us
    unnamed x1, blocking collectives  41.3 us
    all_gather x1, waiting for transfers between devices, shards(): lax.all_gather(fresh_attn, 'rep', axis=0, tiled=True)  30.5 us
    psum x1, blocking collectives, own_squares(): return lax.psum(partial_value, 'shard')  16.5 us
    unnamed x9, local copies, waits for them, and re-layouts  14.2 us
    all_to_all x1, waiting for transfers between devices, shards(): lax.all_to_all(delta_attn[None], 'rep', split_axis=1, concat_axis=0, tile...  14.1 us
    reduce_sum x1, other arithmetic, shards(): jnp.sum(delta_ffn * delta_ffn)  6.13 us
    all_to_all x1, starting transfers between devices, shards(): lax.all_to_all(delta_attn[None], 'rep', split_axis=1, concat_axis=0, tile...  5.19 us
  transfers between devices with their start and end apart: 4, of which 3 were waited for; matrix products, arithmetic and copies ran while one was open for 9% of the time, Pallas kernels for 0%

commit v1 on v0

v1 whole, which is shorter than its diff:
```python
import functools
import math

import jax
import jax.numpy as jnp
from jax import lax
from jax.experimental import pallas as pl
from jax.experimental.pallas import tpu as pltpu
from jax.sharding import PartitionSpec as P

MESH = pl.DeviceIdType.MESH
LANES = 128
SUB = 8


def kernel(cfg, aa, af, la, lf, oa, of, anc_a, anc_f, loc_a, loc_f,
           recv1_0, recv1_1, sum1_0, sum1_1, recv2_0, recv2_1,
           part_own, part_in, fac_own, fac_x, fac_y,
           load_sem, ps, pr, fxs, fxr, fys, fyr,
           s1s, s1r, s2s, s2r, s3s, s3r, s4s, s4r):
    nx, ny, ns, rows, width, chunks, early = cfg
    n = nx * ny
    me_r = lax.axis_index("rep")
    me_s = lax.axis_index("shard")
    x = lax.rem(me_r, nx)
    y = lax.div(me_r, nx)
    loc, anc, out = (loc_a, loc_f), (anc_a, anc_f), (oa, of)
    src = (la, lf)

    def x_peer(i):
        return {"rep": y * nx + i, "shard": me_s}

    def y_peer(i):
        return {"rep": i * nx + x, "shard": me_s}

    def s_peer(i):
        return {"rep": me_r, "shard": i}

    pieces = load_sem.shape[1]
    block = rows // pieces
    loads = []
    for k in range(pieces):
        at = pl.ds(k * block, block)
        for q, (a, b) in enumerate(((la.at[0], loc_a), (lf.at[0], loc_f), (aa, anc_a), (af, anc_f))):
            copy = pltpu.make_async_copy(a.at[at], b.at[at], load_sem.at[q, k])
            copy.start()
            loads.append(copy)

    barrier = pltpu.get_barrier_semaphore()
    for d in range(1, nx):
        pl.semaphore_signal(barrier, inc=1, device_id=x_peer(lax.rem(x + d, nx)), device_id_type=MESH)
    for d in range(1, ny):
        pl.semaphore_signal(barrier, inc=1, device_id=y_peer(lax.rem(y + d, ny)), device_id_type=MESH)
    for d in range(1, ns):
        pl.semaphore_signal(barrier, inc=1, device_id=s_peer(lax.rem(me_s + d, ns)), device_id_type=MESH)
    pl.semaphore_wait(barrier, (nx - 1) + (ny - 1) + (ns - 1))

    paths = (
        (nx, x, x_peer, ny, y, y_peer, recv1_0, sum1_0, recv2_0, fac_x),
        (ny, y, y_peer, nx, x, x_peer, recv1_1, sum1_1, recv2_1, fac_y),
    )
    piece = rows // n

    def remote(a, b, ss, rs, peer):
        return pltpu.make_async_remote_copy(
            src_ref=a, dst_ref=b, send_sem=ss, recv_sem=rs, device_id=peer, device_id_type=MESH)

    def columns(p, c):
        q, col = chunks[p][c]
        return q, pl.ds(col, width), pl.ds(c * width, width)

    count = len(chunks[0])
    stage1, stage2, stage3, stage4 = {}, {}, {}, {}

    def start1(c):
        for p in range(2):
            n1, i1, peer1, n2, i2, peer2, recv1, sum1, recv2, fac = paths[p]
            q, cols, wide = columns(p, c)
            for d in range(1, n1):
                j = lax.rem(i1 + d, n1)
                at = pl.ds(pl.multiple_of(j * (rows // n1), rows // n1), rows // n1)
                copy = remote(src[q].at[0, at, cols], recv1.at[d - 1, :, wide],
                              s1s.at[p, c, d - 1], s1r.at[p, c, d - 1], peer1(j))
                copy.start()
                stage1[p, c, d] = copy

    for c in range(early):
        start1(c)

    accs = tuple(jnp.zeros((SUB, LANES), jnp.float32) for _ in range(4))
    for k in range(pieces):
        for copy in loads[4 * k:4 * k + 4]:
            copy.wait()

        def body(g, accs):
            accs = list(accs)
            at = pl.ds(pl.multiple_of(k * block + g * SUB, SUB), SUB)
            i = 0
            for q in range(2):
                for t in range(loc[q].shape[1] // LANES):
                    lanes = pl.ds(t * LANES, LANES)
                    delta = loc[q][at, lanes] - anc[q][at, lanes]
                    accs[i % 4] = accs[i % 4] + delta * delta
                    i += 1
            return tuple(accs)

        accs = lax.fori_loop(0, block // SUB, body, accs)
    part_own[...] = (accs[0] + accs[1]) + (accs[2] + accs[3])
    sends = []
    for d in range(1, ns):
        copy = remote(part_own, part_in.at[d - 1], ps.at[d - 1], pr.at[d - 1], s_peer(lax.rem(me_s + d, ns)))
        copy.start()
        sends.append(copy)
    total = part_own[...]
    for copy in sends:
        copy.wait_recv()
    for d in range(1, ns):
        total = total + part_in[d - 1]
    squares = jnp.full((SUB, LANES), jnp.sum(total), jnp.float32)
    fac_own[...] = jnp.minimum(jnp.float32(1.0), 1.0 / jnp.sqrt(squares))
    fx, fy = [], []
    for d in range(1, nx):
        copy = remote(fac_own, fac_x.at[d - 1], fxs.at[d - 1], fxr.at[d - 1], x_peer(lax.rem(x + d, nx)))
        copy.start()
        fx.append(copy)
    for d in range(1, ny):
        copy = remote(fac_own, fac_y.at[d - 1], fys.at[d - 1], fyr.at[d - 1], y_peer(lax.rem(y + d, ny)))
        copy.start()
        fy.append(copy)
    for c in range(early, count):
        start1(c)
    for copy in fx + fy:
        copy.wait_recv()

    for c in range(count):
        for p in range(2):
            n1, i1, peer1, n2, i2, peer2, recv1, sum1, recv2, fac = paths[p]
            q, cols, wide = columns(p, c)
            for d in range(1, n1):
                stage1[p, c, d].wait_recv()
            base = i1 * (rows // n1)
            mine = fac_own[...]
            theirs = [fac[d - 1] for d in range(1, n1)]

            def body(g, carry):
                at = pl.ds(pl.multiple_of(base + g * SUB, SUB), SUB)
                to = pl.ds(pl.multiple_of(g * SUB, SUB), SUB)
                col, off = chunks[p][c][1], c * width
                for t in range(width // LANES):
                    here = pl.ds(col + t * LANES, LANES)
                    there = pl.ds(off + t * LANES, LANES)
                    anchor = anc[q][at, here]
                    value = mine * (loc[q][at, here] - anchor)
                    for d in range(1, n1):
                        value = value + theirs[d - 1] * (recv1[d - 1, to, there] - anchor)
                    sum1[to, there] = value
                return carry

            lax.fori_loop(0, rows // n1 // SUB, body, 0)
            for d in range(1, n2):
                j = lax.rem(i2 + d, n2)
                at = pl.ds(pl.multiple_of(j * piece, piece), piece)
                copy = remote(sum1.at[at, wide], recv2.at[d - 1, :, wide],
                              s2s.at[p, c, d - 1], s2r.at[p, c, d - 1], peer2(j))
                copy.start()
                stage2[p, c, d] = copy

    for c in range(count):
        for p in range(2):
            n1, i1, peer1, n2, i2, peer2, recv1, sum1, recv2, fac = paths[p]
            q, cols, wide = columns(p, c)
            for d in range(1, n2):
                stage2[p, c, d].wait_recv()
            own = i2 * piece
            place = i1 * (rows // n1) + own

            def body(g, carry):
                at = pl.ds(pl.multiple_of(own + g * SUB, SUB), SUB)
                to = pl.ds(pl.multiple_of(g * SUB, SUB), SUB)
                dst = pl.ds(pl.multiple_of(place + g * SUB, SUB), SUB)
                col, off = chunks[p][c][1], c * width
                for t in range(width // LANES):
                    there = pl.ds(off + t * LANES, LANES)
                    value = sum1[at, there]
                    for d in range(1, n2):
                        value = value + recv2[d - 1, to, there]
                    out[q][dst, pl.ds(col + t * LANES, LANES)] = value / n
                return carry

            lax.fori_loop(0, piece // SUB, body, 0)
            at = pl.ds(pl.multiple_of(place, piece), piece)
            for d in range(1, n2):
                copy = remote(out[q].at[at, cols], out[q].at[at, cols],
                              s3s.at[p, c, d - 1], s3r.at[p, c, d - 1], peer2(lax.rem(i2 + d, n2)))
                copy.start()
                stage3[p, c, d] = copy

    for c in range(count):
        for p in range(2):
            n1, i1, peer1, n2, i2, peer2, recv1, sum1, recv2, fac = paths[p]
            q, cols, wide = columns(p, c)
            for d in range(1, n2):
                stage3[p, c, d].wait_recv()
            at = pl.ds(pl.multiple_of(i1 * (rows // n1), rows // n1), rows // n1)
            for d in range(1, n1):
                copy = remote(out[q].at[at, cols], out[q].at[at, cols],
                              s4s.at[p, c, d - 1], s4r.at[p, c, d - 1], peer1(lax.rem(i1 + d, n1)))
                copy.start()
                stage4[p, c, d] = copy

    for copy in sends + fx + fy:
        copy.wait_send()
    for stage in (stage1, stage2, stage3):
        for copy in stage.values():
            copy.wait_send()
    for copy in stage4.values():
        copy.wait()


def shards(nx, ny, ns, anchor_attn, anchor_ffn, local_attn, local_ffn):
    rows, da = anchor_attn.shape
    df = anchor_ffn.shape[1]
    width = math.gcd(da // 2, df // 2)
    wide = (da + df) // 2
    chunks = tuple(
        tuple([(1, p * (df // 2) + c) for c in range(0, df // 2, width)]
              + [(0, p * (da // 2) + c) for c in range(0, da // 2, width)])
        for p in range(2))
    count = len(chunks[0])
    early = min(3, count)
    pieces = math.gcd(rows // SUB, 4)
    f32 = jnp.float32
    n = nx * ny
    vmem, dma = pltpu.VMEM, pltpu.SemaphoreType.DMA
    px, py, psh = max(nx - 1, 1), max(ny - 1, 1), max(ns - 1, 1)
    pm = max(px, py)
    scratch = [
        vmem((rows, da), f32), vmem((rows, df), f32), vmem((rows, da), f32), vmem((rows, df), f32),
        vmem((px, rows // nx, wide), f32), vmem((py, rows // ny, wide), f32),
        vmem((rows // nx, wide), f32), vmem((rows // ny, wide), f32),
        vmem((py, rows // n, wide), f32), vmem((px, rows // n, wide), f32),
        vmem((SUB, LANES), f32), vmem((psh, SUB, LANES), f32),
        vmem((SUB, LANES), f32), vmem((px, SUB, LANES), f32), vmem((py, SUB, LANES), f32),
        dma((4, pieces)), dma((psh,)), dma((psh,)),
        dma((px,)), dma((px,)), dma((py,)), dma((py,)),
    ] + [dma((2, count, pm)) for _ in range(8)]
    cfg = (nx, ny, ns, rows, width, chunks, early)
    hbm = pl.BlockSpec(memory_space=pltpu.MemorySpace.HBM)
    vm = pl.BlockSpec(memory_space=pltpu.MemorySpace.VMEM)
    return pl.pallas_call(
        functools.partial(kernel, cfg),
        out_shape=OUT(rows, da, df),
        in_specs=[hbm] * 4,
        out_specs=[vm] * 2,
        scratch_shapes=scratch,
        compiler_params=pltpu.CompilerParams(
            collective_id=0, has_side_effects=True, vmem_limit_bytes=48 * 2**20),
    )(anchor_attn, anchor_ffn, local_attn, local_ffn)


def OUT(rows, da, df):
    return [jax.ShapeDtypeStruct((rows, da), jnp.float32), jax.ShapeDtypeStruct((rows, df), jnp.float32)]


def solution(mesh):
    n = mesh.shape["rep"]
    nx = max(d for d in range(1, math.isqrt(n) + 1) if n % d == 0)
    placed = (P("shard", None), P("shard", None), P("rep", "shard", None), P("rep", "shard", None))
    return jax.shard_map(
        functools.partial(shards, nx, n // nx, mesh.shape["shard"]),
        mesh=mesh,
        in_specs=placed,
        out_specs=(P("shard", None), P("shard", None)),
        check_vma=False,
    )
```

time: 227 us -> 139 us (0.61)
  Pallas kernels: 0 us -> 130 us
  waiting for transfers between devices: 108 us -> 0 us
  blocking collectives: 57.8 us -> 0 us
  between operations: 16 us -> 0.65 us
  local copies, waits for them, and re-layouts: 21.6 us -> 8.32 us
  other arithmetic: 12.5 us -> 0 us
  starting transfers between devices: 10.3 us -> 0 us
    pallas_call x0 -> x1, Pallas kernels: none -> 130 us  [shards(): pl.pallas_call(functools.partial(kernel, cfg), out_shape=OUT(rows, da, df...]
    all_gather x2 -> x0, waiting for transfers between devices: 94.3 us -> none  [the longest x1 63.7 us: shards(): lax.all_gather(fresh_ffn, 'rep', axis=0, tiled=True)]
    unnamed x1 -> x0, blocking collectives: 41.3 us -> none
    psum x1 -> x0, blocking collectives: 16.5 us -> none  [own_squares(): return lax.psum(partial_value, 'shard')]
    all_to_all x2 -> x0, waiting for transfers between devices: 14.1 us -> none  [the longest x1 14.1 us: shards(): lax.all_to_all(delta_attn[None], 'rep', split_axis=1, concat_axis=0, tile...]
    reduce_sum x4 -> x0, other arithmetic: 10.5 us -> none  [the longest x1 6.13 us: shards(): jnp.sum(delta_ffn * delta_ffn)]
    all_to_all x2 -> x0, starting transfers between devices: 10.2 us -> none  [the longest x1 5.19 us: shards(): lax.all_to_all(delta_attn[None], 'rep', split_axis=1, concat_axis=0, tile...]
    broadcast_in_dim x2 -> x0, local copies, waits for them, and re-layouts: 7.36 us -> none  [the longest x1 4.61 us: shards(): delta_ffn[None]]
  transfers between devices with their start and end apart: 4 -> 0, of which waited for: 3 -> 0; matrix products, arithmetic and copies ran while one was open for 9% -> 0% of each run, Pallas kernels for 0% -> 0%
where the time goes in v1:
time: 139 us
  Pallas kernels  130 us (94%)
  local copies, waits for them, and re-layouts  8.32 us (6%)
    pallas_call x1, Pallas kernels, shards(): pl.pallas_call(functools.partial(kernel, cfg), out_shape=OUT(rows, da, df...  130 us
    unnamed x4, local copies, waits for them, and re-layouts  8.32 us

profile of v1, /device:TPU:0, one launch (start us, length us, event | category | flops | bytes accessed | tf_op | source)
XLA Modules:
  0.0 138.6 jit_solution(178020310113809195)
XLA Ops:
  0.6 0.0 copy-start
  0.6 1.6 %copy-done = f32[256,2048]{1,0:T(8,128)S(1)} copy-done((f32[256,2048]{1,0:T(8,128)S(1)}, f32[256,2048]{1,0:T(8,128)}, u32[]{:S(2)}) %copy-start) | copy-done | bytes 2097176
  2.2 129.6 %shard_map.59 = (f32[256,2048]{1,0:T(8,128)S(1)}, f32[256,5120]{1,0:T(8,128)}) custom-call(f32[256,2048]{1,0:T(8,128)S(1)} %copy-done, f32[256,5120]{1,0:T(8,128)} %af.1, f32[1,256,2048]{2,1,0:T(8,128)} %la.1, f32[1,256,5120]{2,1,0:T(8,128)} %lf.1), custom_call_target="tpu_custom_call" | custom-call | tf_op jit(solution)/shard_map/pallas_call | solution.py:250
  131.9 1.3 copy.8
  133.2 5.4 %copy.9 = f32[256,5120]{1,0:T(8,128)} copy(f32[256,5120]{1,0:T(8,128)} %get-tuple-element.5) | data formatting | bytes 10485760
Async XLA Ops:
  0.6 1.6 %copy-start = (f32[256,2048]{1,0:T(8,128)S(1)}, f32[256,2048]{1,0:T(8,128)}, u32[]{:S(2)}) copy-start(f32[256,2048]{1,0:T(8,128)} %aa.1) | copy-start | bytes 6291460

commit v2 on v1

--- a/solution.py
+++ b/solution.py
@@ -254,12 +254,12 @@
         out_specs=[vm] * 2,
         scratch_shapes=scratch,
         compiler_params=pltpu.CompilerParams(
-            collective_id=0, has_side_effects=True, vmem_limit_bytes=48 * 2**20),
+            collective_id=0, has_side_effects=True, vmem_limit_bytes=52 * 2**20),
     )(anchor_attn, anchor_ffn, local_attn, local_ffn)
 
 
 def OUT(rows, da, df):
-    return [jax.ShapeDtypeStruct((rows, da), jnp.float32), jax.ShapeDtypeStruct((rows, df), jnp.float32)]
+    return [pltpu.VMEM((rows, da), jnp.float32), pltpu.VMEM((rows, df), jnp.float32)]
 
 
 def solution(mesh):

time: 139 us -> 132 us (0.950)
  local copies, waits for them, and re-layouts: 8.32 us -> 3.68 us
  Pallas kernels: 130 us -> 127 us
    unnamed x4 -> x2, local copies, waits for them, and re-layouts: 8.32 us -> 3.68 us
    pallas_call x1, Pallas kernels: 130 us -> 127 us  [shards(): pl.pallas_call(functools.partial(kernel, cfg), out_shape=OUT(rows, da, df...]
where the time goes in v2:
time: 132 us
  Pallas kernels  127 us (96%)
  local copies, waits for them, and re-layouts  3.68 us (3%)
    pallas_call x1, Pallas kernels, shards(): pl.pallas_call(functools.partial(kernel, cfg), out_shape=OUT(rows, da, df...  127 us
    unnamed x2, local copies, waits for them, and re-layouts  3.68 us

profile of v2, /device:TPU:0, one launch (start us, length us, event | category | flops | bytes accessed | tf_op | source)
XLA Modules:
  0.0 131.6 jit_solution(16543678049020546099)
XLA Ops:
  0.6 127.2 %shard_map.59 = (f32[256,2048]{1,0:T(8,128)S(1)}, f32[256,5120]{1,0:T(8,128)S(1)}) custom-call(f32[256,2048]{1,0:T(8,128)} %aa.1, f32[256,5120]{1,0:T(8,128)} %af.1, f32[1,256,2048]{2,1,0:T(8,128)} %la.1, f32[1,256,5120]{2,1,0:T(8,128)} %lf.1), custom_call_target="tpu_custom_call" | custom-call | tf_op jit(solution)/shard_map/pallas_call | solution.py:250
  127.9 1.3 %copy.8 = f32[256,2048]{1,0:T(8,128)} copy(f32[256,2048]{1,0:T(8,128)S(1)} %get-tuple-element.2) | data formatting | bytes 4194304
  129.2 2.4 %copy.9 = f32[256,5120]{1,0:T(8,128)} copy(f32[256,5120]{1,0:T(8,128)S(1)} %get-tuple-element.3) | data formatting | bytes 10485760

commit v3 on v2

--- a/solution.py
+++ b/solution.py
@@ -15,7 +15,7 @@
 
 def kernel(cfg, aa, af, la, lf, oa, of, anc_a, anc_f, loc_a, loc_f,
            recv1_0, recv1_1, sum1_0, sum1_1, recv2_0, recv2_1,
-           part_own, part_in, fac_own, fac_x, fac_y,
+           part_own, part_up, part_down, part_in, fac_own, fac_x, fac_y,
            load_sem, ps, pr, fxs, fxr, fys, fyr,
            s1s, s1r, s2s, s2r, s3s, s3r, s4s, s4r):
     nx, ny, ns, rows, width, chunks, early = cfg
@@ -46,14 +46,25 @@
             copy.start()
             loads.append(copy)
 
+    part_in[...] = jnp.zeros_like(part_in)
+
+    has_next, has_prev = me_s < ns - 1, me_s > 0
     barrier = pltpu.get_barrier_semaphore()
+
+    @pl.when(has_next)
+    def _():
+        pl.semaphore_signal(barrier, inc=1, device_id=s_peer(me_s + 1), device_id_type=MESH)
+
+    @pl.when(has_prev)
+    def _():
+        pl.semaphore_signal(barrier, inc=1, device_id=s_peer(me_s - 1), device_id_type=MESH)
+
     for d in range(1, nx):
         pl.semaphore_signal(barrier, inc=1, device_id=x_peer(lax.rem(x + d, nx)), device_id_type=MESH)
     for d in range(1, ny):
         pl.semaphore_signal(barrier, inc=1, device_id=y_peer(lax.rem(y + d, ny)), device_id_type=MESH)
-    for d in range(1, ns):
-        pl.semaphore_signal(barrier, inc=1, device_id=s_peer(lax.rem(me_s + d, ns)), device_id_type=MESH)
-    pl.semaphore_wait(barrier, (nx - 1) + (ny - 1) + (ns - 1))
+    near = jnp.where(has_next, 1, 0) + jnp.where(has_prev, 1, 0)
+    pl.semaphore_wait(barrier, (nx - 1) + (ny - 1) + near)
 
     paths = (
         (nx, x, x_peer, ny, y, y_peer, recv1_0, sum1_0, recv2_0, fac_x),
@@ -106,16 +117,42 @@
 
         accs = lax.fori_loop(0, block // SUB, body, accs)
     part_own[...] = (accs[0] + accs[1]) + (accs[2] + accs[3])
-    sends = []
-    for d in range(1, ns):
-        copy = remote(part_own, part_in.at[d - 1], ps.at[d - 1], pr.at[d - 1], s_peer(lax.rem(me_s + d, ns)))
-        copy.start()
-        sends.append(copy)
-    total = part_own[...]
-    for copy in sends:
-        copy.wait_recv()
-    for d in range(1, ns):
-        total = total + part_in[d - 1]
+    up = remote(part_up, part_in.at[0], ps.at[0], pr.at[0], s_peer(lax.rem(me_s + 1, ns)))
+    down = remote(part_down, part_in.at[1], ps.at[1], pr.at[1], s_peer(lax.rem(me_s + ns - 1, ns)))
+
+    def pass_up():
+        @pl.when(has_prev)
+        def _():
+            up.wait_recv()
+
+        part_up[...] = part_own[...] + part_in[0]
+
+        @pl.when(has_next)
+        def _():
+            up.start()
+
+    def pass_down():
+        @pl.when(has_next)
+        def _():
+            down.wait_recv()
+
+        part_down[...] = part_own[...] + part_in[1]
+
+        @pl.when(has_prev)
+        def _():
+            down.start()
+
+    @pl.when(me_s < ns // 2)
+    def _():
+        pass_up()
+        pass_down()
+
+    @pl.when(me_s >= ns // 2)
+    def _():
+        pass_down()
+        pass_up()
+
+    total = part_own[...] + (part_in[0] + part_in[1])
     squares = jnp.full((SUB, LANES), jnp.sum(total), jnp.float32)
     fac_own[...] = jnp.minimum(jnp.float32(1.0), 1.0 / jnp.sqrt(squares))
     fx, fy = [], []
@@ -208,7 +245,15 @@
                 copy.start()
                 stage4[p, c, d] = copy
 
-    for copy in sends + fx + fy:
+    @pl.when(has_next)
+    def _():
+        up.wait_send()
+
+    @pl.when(has_prev)
+    def _():
+        down.wait_send()
+
+    for copy in fx + fy:
         copy.wait_send()
     for stage in (stage1, stage2, stage3):
         for copy in stage.values():
@@ -227,27 +272,27 @@
               + [(0, p * (da // 2) + c) for c in range(0, da // 2, width)])
         for p in range(2))
     count = len(chunks[0])
-    early = min(3, count)
+    early = min(4, count)
     pieces = math.gcd(rows // SUB, 4)
     f32 = jnp.float32
     n = nx * ny
     vmem, dma = pltpu.VMEM, pltpu.SemaphoreType.DMA
-    px, py, psh = max(nx - 1, 1), max(ny - 1, 1), max(ns - 1, 1)
+    px, py = max(nx - 1, 1), max(ny - 1, 1)
     pm = max(px, py)
     scratch = [
         vmem((rows, da), f32), vmem((rows, df), f32), vmem((rows, da), f32), vmem((rows, df), f32),
         vmem((px, rows // nx, wide), f32), vmem((py, rows // ny, wide), f32),
         vmem((rows // nx, wide), f32), vmem((rows // ny, wide), f32),
         vmem((py, rows // n, wide), f32), vmem((px, rows // n, wide), f32),
-        vmem((SUB, LANES), f32), vmem((psh, SUB, LANES), f32),
+        vmem((SUB, LANES), f32), vmem((SUB, LANES), f32), vmem((SUB, LANES), f32), vmem((2, SUB, LANES), f32),
         vmem((SUB, LANES), f32), vmem((px, SUB, LANES), f32), vmem((py, SUB, LANES), f32),
-        dma((4, pieces)), dma((psh,)), dma((psh,)),
+        dma((4, pieces)), dma((2,)), dma((2,)),
         dma((px,)), dma((px,)), dma((py,)), dma((py,)),
     ] + [dma((2, count, pm)) for _ in range(8)]
     cfg = (nx, ny, ns, rows, width, chunks, early)
     hbm = pl.BlockSpec(memory_space=pltpu.MemorySpace.HBM)
     vm = pl.BlockSpec(memory_space=pltpu.MemorySpace.VMEM)
-    return pl.pallas_call(
+    out = pl.pallas_call(
         functools.partial(kernel, cfg),
         out_shape=OUT(rows, da, df),
         in_specs=[hbm] * 4,
@@ -256,6 +301,33 @@
         compiler_params=pltpu.CompilerParams(
             collective_id=0, has_side_effects=True, vmem_limit_bytes=52 * 2**20),
     )(anchor_attn, anchor_ffn, local_attn, local_ffn)
+    return write_out(*out)
+
+
+def write_kernel(a, b, oa, ob, sem):
+    pieces = sem.shape[1]
+    block = a.shape[0] // pieces
+    copies = []
+    for k in range(pieces):
+        at = pl.ds(k * block, block)
+        for q, (src, dst) in enumerate(((b, ob), (a, oa))):
+            copy = pltpu.make_async_copy(src.at[at], dst.at[at], sem.at[q, k])
+            copy.start()
+            copies.append(copy)
+    for copy in copies:
+        copy.wait()
+
+
+def write_out(a, b):
+    pieces = math.gcd(a.shape[0] // SUB, 4)
+    return pl.pallas_call(
+        write_kernel,
+        out_shape=[jax.ShapeDtypeStruct(v.shape, v.dtype) for v in (a, b)],
+        in_specs=[pl.BlockSpec(memory_space=pltpu.MemorySpace.VMEM)] * 2,
+        out_specs=[pl.BlockSpec(memory_space=pltpu.MemorySpace.HBM)] * 2,
+        scratch_shapes=[pltpu.SemaphoreType.DMA((2, pieces))],
+        compiler_params=pltpu.CompilerParams(vmem_limit_bytes=16 * 2**20),
+    )(a, b)
 
 
 def OUT(rows, da, df):

time: 132 us -> 129 us (0.977)
  local copies, waits for them, and re-layouts: 3.68 us -> 0 us
    unnamed x2 -> x0, local copies, waits for them, and re-layouts: 3.68 us -> none
    pallas_call x0 -> x1, Pallas kernels: none -> 3.05 us  [write_out(): pl.pallas_call(write_kernel, out_shape=[jax.ShapeDtypeStruct(v.shape, v.d...]
    pallas_call x1, Pallas kernels: 127 us -> 125 us  [shards(): pl.pallas_call(functools.partial(kernel, cfg), out_shape=OUT(rows, da, df...]
where the time goes in v3:
time: 129 us
  Pallas kernels  128 us (99%)
    pallas_call x1, Pallas kernels, shards(): pl.pallas_call(functools.partial(kernel, cfg), out_shape=OUT(rows, da, df...  125 us
    pallas_call x1, Pallas kernels, write_out(): pl.pallas_call(write_kernel, out_shape=[jax.ShapeDtypeStruct(v.shape, v.d...  3.05 us

profile of v3, /device:TPU:0, one launch (start us, length us, event | category | flops | bytes accessed | tf_op | source)
XLA Modules:
  0.0 128.8 jit_solution(11963058930279592787)
XLA Ops:
  0.6 125.1 %shard_map.59 = (f32[256,2048]{1,0:T(8,128)S(1)}, f32[256,5120]{1,0:T(8,128)S(1)}) custom-call(f32[256,2048]{1,0:T(8,128)} %aa.1, f32[256,5120]{1,0:T(8,128)} %af.1, f32[1,256,2048]{2,1,0:T(8,128)} %la.1, f32[1,256,5120]{2,1,0:T(8,128)} %lf.1), custom_call_target="tpu_custom_call" | custom-call | tf_op jit(solution)/shard_map/pallas_call | solution.py:295
  125.7 3.1 %shard_map.60 = (f32[256,2048]{1,0:T(8,128)}, f32[256,5120]{1,0:T(8,128)}) custom-call(f32[256,2048]{1,0:T(8,128)S(1)} %get-tuple-element.4.a, f32[256,5120]{1,0:T(8,128)S(1)} %get-tuple-element.5.b), custom_call_target="tpu_custom_call" | custom-call | tf_op jit(solution)/shard_map/pallas_call | solution.py:323

commit v4 on v3

--- a/solution.py
+++ b/solution.py
@@ -36,16 +36,6 @@
     def s_peer(i):
         return {"rep": me_r, "shard": i}
 
-    pieces = load_sem.shape[1]
-    block = rows // pieces
-    loads = []
-    for k in range(pieces):
-        at = pl.ds(k * block, block)
-        for q, (a, b) in enumerate(((la.at[0], loc_a), (lf.at[0], loc_f), (aa, anc_a), (af, anc_f))):
-            copy = pltpu.make_async_copy(a.at[at], b.at[at], load_sem.at[q, k])
-            copy.start()
-            loads.append(copy)
-
     part_in[...] = jnp.zeros_like(part_in)
 
     has_next, has_prev = me_s < ns - 1, me_s > 0
@@ -95,7 +85,19 @@
                 copy.start()
                 stage1[p, c, d] = copy
 
-    for c in range(early):
+    start1(0)
+
+    pieces = load_sem.shape[1]
+    block = rows // pieces
+    loads = []
+    for k in range(pieces):
+        at = pl.ds(k * block, block)
+        for q, (a, b) in enumerate(((la.at[0], loc_a), (lf.at[0], loc_f), (aa, anc_a), (af, anc_f))):
+            copy = pltpu.make_async_copy(a.at[at], b.at[at], load_sem.at[q, k])
+            copy.start()
+            loads.append(copy)
+
+    for c in range(1, early):
         start1(c)
 
     accs = tuple(jnp.zeros((SUB, LANES), jnp.float32) for _ in range(4))

time: 129 us -> 129 us (level)
  no operation moved by 1% of the time
where the time goes in v4:
time: 129 us
  Pallas kernels  128 us (99%)
    pallas_call x1, Pallas kernels, shards(): pl.pallas_call(functools.partial(kernel, cfg), out_shape=OUT(rows, da, df...  125 us
    pallas_call x1, Pallas kernels, write_out(): pl.pallas_call(write_kernel, out_shape=[jax.ShapeDtypeStruct(v.shape, v.d...  3.05 us

profile of v4, /device:TPU:0, one launch (start us, length us, event | category | flops | bytes accessed | tf_op | source)
XLA Modules:
  0.0 128.8 jit_solution(9468594067453620471)
XLA Ops:
  0.6 125.1 %shard_map.59 = (f32[256,2048]{1,0:T(8,128)S(1)}, f32[256,5120]{1,0:T(8,128)S(1)}) custom-call(f32[256,2048]{1,0:T(8,128)} %aa.1, f32[256,5120]{1,0:T(8,128)} %af.1, f32[1,256,2048]{2,1,0:T(8,128)} %la.1, f32[1,256,5120]{2,1,0:T(8,128)} %lf.1), custom_call_target="tpu_custom_call" | custom-call | tf_op jit(solution)/shard_map/pallas_call | solution.py:297
  125.7 3.1 %shard_map.60 = (f32[256,2048]{1,0:T(8,128)}, f32[256,5120]{1,0:T(8,128)}) custom-call(f32[256,2048]{1,0:T(8,128)S(1)} %get-tuple-element.4.a, f32[256,5120]{1,0:T(8,128)S(1)} %get-tuple-element.5.b), custom_call_target="tpu_custom_call" | custom-call | tf_op jit(solution)/shard_map/pallas_call | solution.py:325

commit v5 on v4

--- a/solution.py
+++ b/solution.py
@@ -268,13 +268,14 @@
     rows, da = anchor_attn.shape
     df = anchor_ffn.shape[1]
     width = math.gcd(da // 2, df // 2)
+    width = width // 2 if width % (2 * LANES) == 0 else width
     wide = (da + df) // 2
     chunks = tuple(
         tuple([(1, p * (df // 2) + c) for c in range(0, df // 2, width)]
               + [(0, p * (da // 2) + c) for c in range(0, da // 2, width)])
         for p in range(2))
     count = len(chunks[0])
-    early = min(4, count)
+    early = min(8, count)
     pieces = math.gcd(rows // SUB, 4)
     f32 = jnp.float32
     n = nx * ny

time: 129 us -> 130 us (level)
  no operation moved by 1% of the time
where the time goes in v5:
time: 130 us
  Pallas kernels  129 us (99%)
    pallas_call x1, Pallas kernels, shards(): pl.pallas_call(functools.partial(kernel, cfg), out_shape=OUT(rows, da, df...  126 us
    pallas_call x1, Pallas kernels, write_out(): pl.pallas_call(write_kernel, out_shape=[jax.ShapeDtypeStruct(v.shape, v.d...  3.05 us

profile of v5, /device:TPU:0, one launch (start us, length us, event | category | flops | bytes accessed | tf_op | source)
XLA Modules:
  0.0 129.8 jit_solution(15496318866852133985)
XLA Ops:
  0.6 126.1 %shard_map.59 = (f32[256,2048]{1,0:T(8,128)S(1)}, f32[256,5120]{1,0:T(8,128)S(1)}) custom-call(f32[256,2048]{1,0:T(8,128)} %aa.1, f32[256,5120]{1,0:T(8,128)} %af.1, f32[1,256,2048]{2,1,0:T(8,128)} %la.1, f32[1,256,5120]{2,1,0:T(8,128)} %lf.1), custom_call_target="tpu_custom_call" | custom-call | tf_op jit(solution)/shard_map/pallas_call | solution.py:298
  126.7 3.1 %shard_map.60 = (f32[256,2048]{1,0:T(8,128)}, f32[256,5120]{1,0:T(8,128)}) custom-call(f32[256,2048]{1,0:T(8,128)S(1)} %get-tuple-element.4.a, f32[256,5120]{1,0:T(8,128)S(1)} %get-tuple-element.5.b), custom_call_target="tpu_custom_call" | custom-call | tf_op jit(solution)/shard_map/pallas_call | solution.py:326
